TPU v7x, 512 devices: a whole 4x4x16 slice. The times are simulated.
512 devices in a mesh: expert: 32 (over z, x_lo), fsdp: 16 (over x_hi, y, core).
Axes of the slice: x: 4 (x_hi: 2, x_lo: 2; x = x_hi * 2 + x_lo), y: 4, z: 16, core: 2. Of those that a mesh axis runs over, the one named last changes fastest.
Arguments:
- tokens: bfloat16 [3584, 4096], P(('expert', 'fsdp')), may hold values from -6 to 6
- expert_ids: int32 [3584, 8], P(('expert', 'fsdp')), may hold values from 0 to 31, all different within a row; in each aligned block of 7 rows (0 to 6, 7 to 13, ...) at most 2 rows name the same one
- gate_scores: float32 [3584, 8], P(('expert', 'fsdp')), may hold values from 0.05 to 1
- w_gate: bfloat16 [32, 1536, 4096], P('expert', 'fsdp'), may hold values from -0.09375 to 0.09375
- w_up: bfloat16 [32, 1536, 4096], P('expert', 'fsdp'), may hold values from -0.09375 to 0.09375
- w_down: bfloat16 [32, 1536, 4096], P('expert', None, 'fsdp'), may hold values from -0.15625 to 0.15625
Outputs:
- mixed: bfloat16 [3584, 4096], P(('expert', 'fsdp'))
Inputs may be any that keep to these rules, and one draw needn't show every extreme that they name: `expert_ids`: each token names 8 different experts. Within the 7 tokens of one device (aligned blocks of rows) no expert is named more than 2 times, and in every draw some expert is named exactly 2 times in some block.
All inputs are finite; a program needn't handle non-finite values.
Results may differ from a plain program's by a relative error of at most 0.0057.
Values may be sent and summed in bfloat16 or wider, within the bound.
A program may use at most 64 MiB of HBM per device.

v0:
```python
import jax
import jax.numpy as jnp
from jax import lax
from jax.sharding import PartitionSpec as P


def on_device(tokens, expert_ids, gate_scores, w_gate, w_up, w_down):
    n_expert = lax.axis_size("expert")
    n_fsdp = lax.axis_size("fsdp")
    local_tok, top_k = expert_ids.shape
    per_column = w_gate.shape[0]
    experts = per_column * n_expert
    capacity = min(local_tok, max(2, 3 * local_tok * top_k // (2 * experts)))
    width = tokens.shape[1]
    feature_cols = w_down.shape[2]
    weights = gate_scores / jnp.sum(gate_scores, axis=1, keepdims=True)
    expert_iota = lax.broadcasted_iota(jnp.int32, (1, 1, experts), 2)
    matches = (expert_ids[:, :, None] == expert_iota).astype(jnp.int32)
    chosen = jnp.sum(matches, axis=1, dtype=jnp.int32)
    weight_table = jnp.sum(weights[:, :, None] * matches.astype(jnp.float32), axis=1)
    ranks = jnp.cumsum(chosen, axis=0, dtype=jnp.int32) - chosen
    slot_iota = lax.broadcasted_iota(jnp.int32, (1, 1, capacity), 2)
    slot_mask = jnp.logical_and(ranks[:, :, None] == slot_iota, chosen[:, :, None] > 0)
    select_f32 = jnp.transpose(slot_mask.astype(jnp.float32), (1, 2, 0))
    select_bf = select_f32.astype(jnp.bfloat16)
    combine_table = select_f32 * jnp.transpose(weight_table)[:, None, :]
    outgoing = jnp.einsum("ect,td->ecd", select_bf, tokens, preferred_element_type=jnp.float32)
    outgoing = outgoing.astype(jnp.bfloat16)
    arrived = lax.all_to_all(outgoing, "expert", split_axis=0, concat_axis=0, tiled=True)
    portion = lax.all_gather(arrived[None], "fsdp", axis=0, tiled=True)
    routed = portion.reshape(portion.shape[0], n_expert, per_column, capacity, width)
    gate_act = jnp.einsum("knjcd,jhd->knjch", routed, w_gate, preferred_element_type=jnp.float32)
    up_act = jnp.einsum("knjcd,jhd->knjch", routed, w_up, preferred_element_type=jnp.float32)
    hidden = (jax.nn.silu(gate_act) * up_act).astype(jnp.bfloat16)
    summed = jnp.einsum(
        "fnjch,jhd->fnjcd",
        lax.all_gather(hidden, "fsdp", axis=4, tiled=True),
        w_down,
        preferred_element_type=jnp.float32,
    )
    expert_out = summed.astype(jnp.bfloat16).reshape(
        n_fsdp, n_expert, per_column * capacity, feature_cols
    )
    returned = lax.all_to_all(
        lax.all_to_all(expert_out, "expert", split_axis=1, concat_axis=1, tiled=True),
        "fsdp",
        split_axis=0,
        concat_axis=3,
        tiled=True,
    )
    returned = returned.reshape(experts, capacity, width)
    mixed = jnp.einsum(
        "ect,ecd->td", combine_table, returned.astype(jnp.float32), precision=lax.Precision.HIGHEST
    )
    return mixed.astype(jnp.bfloat16)


def solution(mesh):
    placed = (
        P(("expert", "fsdp"), None),
        P(("expert", "fsdp"), None),
        P(("expert", "fsdp"), None),
        P("expert", "fsdp", None),
        P("expert", "fsdp", None),
        P("expert", None, "fsdp"),
    )
    return jax.shard_map(
        on_device,
        mesh=mesh,
        in_specs=placed,
        out_specs=P(("expert", "fsdp"), None),
        check_vma=False,
    )
```

profile of v0, /device:TPU:1, one launch (start us, length us, event | category | flops | bytes accessed | tf_op | source)
XLA Modules:
  0.0 343.0 jit_solution(12220957122521888835)
XLA Ops:
  6.5 0.0 copy-start
  6.5 0.0 all-gather.6.cloned.1.call-start
  6.5 0.8 convert_reduce_fusion
  7.4 1.2 convolution_convert_fusion
  8.6 0.5 copy.34
  9.2 48.1 %all_to_all.25 = bf16[32,2,4096]{2,1,0:T(2,128)(2,1)S(1)} all-to-all(bf16[32,2,4096]{2,1,0:T(2,128)(2,1)S(1)} %copy.34), channel_id=1, replica_groups=mesh['expert'=32,'fsdp'=16] {'expert'}, dimensions={0} | all-to-all | bytes 1048576 | tf_op jit(solution)/shard_map/all_to_all | solution.py:29
  57.3 1.1 copy.35
  58.4 0.0 all-gather.6.cloned.1.call-update
  58.4 0.0 all-gather.4.cloned.1.call-start
  58.5 82.3 %all-gather.6.cloned.1.call-done = bf16[512,2,4096]{2,0,1:T(8,128)(2,1)} async-done(((bf16[32,2,4096]{2,0,1:T(8,128)(2,1)}), bf16[512,2,4096]{2,0,1:T(8,128)(2,1)}) %all-gather.6.cloned.1.call-update) | async-done | bytes 8388624 | tf_op jit(solution)/shard_map/all_gather | solution.py:30
  140.8 0.0 copy-start.3
  140.8 0.0 copy-start.4
  140.8 6.0 %fusion.10 = f32[16,32,1,2,96]{4,1,3,0,2:T(8,128)S(1)} fusion(bf16[16,32,2,4096]{3,1,0,2:T(8,128)(2,1)} %bitcast.65, bf16[1,96,4096]{2,1,0:T(8,128)(2,1)} %param.9), kind=kOutput, calls=%fused_computation.10 | convolution fusion | flops 805306368 | bytes 9568256 | tf_op jit(solution)/shard_map/knjcd,jhd->knjch/dot_general | solution.py:32
  146.8 0.0 copy-done.3
  146.8 0.1 copy-done.4
  146.9 2.3 fusion.19
  149.3 2.1 copy.38
  151.3 0.0 all-gather.4.cloned.1.call-update
  151.4 103.8 %all-gather.4.cloned.1.call-done = bf16[16,32,1,2,1536]{1,0,3,2,4:T(8,128)(2,1)} async-done(((bf16[16,32,1,2,96]{1,0,3,2,4:T(8,128)(2,1)}), bf16[16,32,1,2,1536]{1,0,3,2,4:T(8,128)(2,1)}) %all-gather.4.cloned.1.call-update) | async-done | bytes 3145744 | tf_op jit(solution)/shard_map/all_gather | solution.py:37
  255.2 13.4 %copy.39 = bf16[16,32,1,2,1536]{4,1,3,0,2:T(8,128)(2,1)} copy(bf16[16,32,1,2,1536]{1,0,3,2,4:T(8,128)(2,1)} %all-gather.4.cloned.1.call-done) | data formatting | bytes 6291456 | tf_op jit(solution)/shard_map/all_gather | solution.py:37
  268.6 0.0 copy-done
  268.6 0.0 copy-start.2
  268.6 0.0 copy-start.1
  268.6 2.9 fusion.7
  271.5 0.5 copy.40
  272.0 44.3 %all_to_all.26 = bf16[16,32,2,256]{3,2,0,1:T(2,128)(2,1)S(1)} all-to-all(bf16[16,32,2,256]{3,2,0,1:T(2,128)(2,1)S(1)} %copy.40), channel_id=1, replica_groups=mesh['expert'=32,'fsdp'=16] {'expert'}, dimensions={1} | all-to-all | bytes 1048576 | tf_op jit(solution)/shard_map/all_to_all | solution.py:45
  316.4 1.3 copy.41
  317.7 5.8 %all-to-all-start.2 = ((bf16[16,32,2,256]{3,2,1,0:T(2,128)(2,1)}), bf16[16,32,2,256]{3,2,1,0:T(2,128)(2,1)S(1)}, u32[]{:S(2)}, u32[]{:S(2)}) async-start(bf16[16,32,2,256]{3,2,1,0:T(2,128)(2,1)} %copy.41), calls=%async_computation.2 | async-start | bytes 1048576 | tf_op jit(solution)/shard_map/all_to_all | solution.py:44
  323.4 0.0 copy-done.2
  323.4 0.1 reduce_sum.28
  323.6 0.1 broadcast_divide_fusion
  323.6 0.0 copy-done.1
  323.6 0.1 fusion.27
  323.7 10.9 %all-to-all-done.2 = bf16[16,32,2,256]{3,2,1,0:T(2,128)(2,1)S(1)} async-done(((bf16[16,32,2,256]{3,2,1,0:T(2,128)(2,1)}), bf16[16,32,2,256]{3,2,1,0:T(2,128)(2,1)S(1)}, u32[]{:S(2)}, u32[]{:S(2)}) %all-to-all-start.2) | async-done | bytes 524320 | tf_op jit(solution)/shard_map/all_to_all | solution.py:44
  334.6 0.3 copy.42
  334.9 0.2 reshape.47
  335.2 1.0 fusion.4
  (3 shorter events, 0.0 us)
Async XLA Ops:
  6.5 262.1 %copy-start = (bf16[1,1536,256]{2,1,0:T(8,128)(2,1)S(1)}, bf16[1,1536,256]{2,1,0:T(8,128)(2,1)}, u32[]{:S(2)}) copy-start(bf16[1,1536,256]{2,1,0:T(8,128)(2,1)} %param.11) | copy-start | bytes 2359300
  6.5 134.3 %all-gather.6.cloned.1.call-start = ((), (), s32[]{:S(2)}) async-start(), calls=%async_computation.4 | async-start | bytes 8912896 | tf_op jit(solution)/shard_map/all_gather | solution.py:30
  58.4 196.7 %all-gather.4.cloned.1.call-start = ((), (), s32[]{:S(2)}) async-start(), calls=%async_computation.3 | async-start | bytes 13369344 | tf_op jit(solution)/shard_map/all_gather | solution.py:37
  140.8 6.0 %copy-start.3 = (bf16[512,2,4096]{2,0,1:T(8,128)(2,1)S(1)}, bf16[512,2,4096]{2,0,1:T(8,128)(2,1)}, u32[]{:S(2)}) copy-start(bf16[512,2,4096]{2,0,1:T(8,128)(2,1)} %all-gather.6.cloned.1.call-done) | copy-start | bytes 25165828
  140.8 6.1 %copy-start.4 = (bf16[1,96,4096]{2,1,0:T(8,128)(2,1)S(1)}, bf16[1,96,4096]{2,1,0:T(8,128)(2,1)}, u32[]{:S(2)}) copy-start(bf16[1,96,4096]{2,1,0:T(8,128)(2,1)} %param.10) | copy-start | bytes 2359300
  268.6 54.9 %copy-start.2 = (f32[7,8]{1,0:T(8,128)S(1)}, f32[7,8]{1,0:T(8,128)}, u32[]{:S(2)}) copy-start(f32[7,8]{1,0:T(8,128)} %param.8) | copy-start | bytes 676
  268.6 55.1 %copy-start.1 = (s32[7,8]{1,0:T(8,128)S(1)}, s32[7,8]{1,0:T(8,128)}, u32[]{:S(2)}) copy-start(s32[7,8]{1,0:T(8,128)} %param.7) | copy-start | bytes 676
  317.7 16.9 %all-to-all-start.2 = ((bf16[16,32,2,256]{3,2,1,0:T(2,128)(2,1)}), bf16[16,32,2,256]{3,2,1,0:T(2,128)(2,1)S(1)}, u32[]{:S(2)}, u32[]{:S(2)}) async-start(bf16[16,32,2,256]{3,2,1,0:T(2,128)(2,1)} %copy.41), calls=%async_computation.2 | async-start | bytes 1048576 | tf_op jit(solution)/shard_map/all_to_all | solution.py:44
Sparse Core Ops, SparseCore 0:
  58.6 82.1 all-gather.5
  151.5 103.6 all-gather.3
where the time goes:
time: 344 us; the launch traced here: 343 us
  waiting for transfers between devices  197 us (57%)
  blocking collectives  92.5 us (27%)
  local copies, waits for them, and re-layouts  19.6 us (6%)
  between operations  13.5 us (4%)
  matrix products  13.4 us (4%)
  starting transfers between devices  5.81 us (2%)
    all_gather x1, waiting for transfers between devices, on_device(): lax.all_gather(hidden, 'fsdp', axis=4, tiled=True)  104 us
    all_gather x1, waiting for transfers between devices, on_device(): portion = lax.all_gather(arrived[None], 'fsdp', axis=0, tiled=True)  82.3 us
    all_to_all x1, blocking collectives, on_device(): lax.all_to_all(outgoing, 'expert', split_axis=0, concat_axis=0, tiled=True)  48.1 us
    all_to_all x1, blocking collectives, on_device(): lax.all_to_all(expert_out, 'expert', split_axis=1, concat_axis=1, tiled=T...  44.3 us
    all_gather x1, local copies, waits for them, and re-layouts, on_device(): lax.all_gather(hidden, 'fsdp', axis=4, tiled=True)  13.4 us
    all_to_all x1, waiting for transfers between devices, on_device(): lax.all_to_all(lax.all_to_all(expert_out, 'expert', split_axis=1, concat_...  10.9 us
  transfers between devices with their start and end apart: 3, of which 3 were waited for; matrix products, arithmetic and copies ran while one was open for 0% of the time, Pallas kernels for 0%

commit v1 on v0

--- a/solution.py
+++ b/solution.py
@@ -2,6 +2,7 @@
 import jax.numpy as jnp
 from jax import lax
 from jax.sharding import PartitionSpec as P
+from jax.lax import all_to_all, psum
 
 
 def on_device(tokens, expert_ids, gate_scores, w_gate, w_up, w_down):
@@ -41,12 +42,10 @@
     expert_out = summed.astype(jnp.bfloat16).reshape(
         n_fsdp, n_expert, per_column * capacity, feature_cols
     )
-    returned = lax.all_to_all(
-        lax.all_to_all(expert_out, "expert", split_axis=1, concat_axis=1, tiled=True),
-        "fsdp",
-        split_axis=0,
-        concat_axis=3,
-        tiled=True,
+    q_in = lax.all_to_all(expert_out, "expert", split_axis=1, concat_axis=1, tiled=True)
+    returned = jnp.concatenate(
+        all_to_all(jnp.stack(jnp.split(q_in, psum(1, "fsdp"), axis=0), axis=0), "fsdp", 0, 0),
+        axis=3,
     )
     returned = returned.reshape(experts, capacity, width)
     mixed = jnp.einsum(

time: 344 us -> 352 us (1.023)
  local copies, waits for them, and re-layouts: 19.6 us -> 28.4 us
    unnamed x10 -> x25, local copies, waits for them, and re-layouts: 0.13 us -> 9.57 us
where the time goes in v1:
time: 352 us
  waiting for transfers between devices  197 us (56%)
  blocking collectives  92.5 us (26%)
  local copies, waits for them, and re-layouts  28.4 us (8%)
  between operations  13.5 us (4%)
  matrix products  13.4 us (4%)
  starting transfers between devices  5.81 us (2%)
    all_gather x1, waiting for transfers between devices, on_device(): lax.all_gather(hidden, 'fsdp', axis=4, tiled=True)  104 us
    all_gather x1, waiting for transfers between devices, on_device(): portion = lax.all_gather(arrived[None], 'fsdp', axis=0, tiled=True)  82.3 us
    all_to_all x1, blocking collectives, on_device(): lax.all_to_all(outgoing, 'expert', split_axis=0, concat_axis=0, tiled=True)  48.1 us
    all_to_all x1, blocking collectives, on_device(): lax.all_to_all(expert_out, 'expert', split_axis=1, concat_axis=1, tiled=T...  44.3 us
    all_gather x1, local copies, waits for them, and re-layouts, on_device(): lax.all_gather(hidden, 'fsdp', axis=4, tiled=True)  13.4 us
    all_to_all x1, waiting for transfers between devices, on_device(): all_to_all(jnp.stack(jnp.split(q_in, psum(1, 'fsdp'), axis=0), axis=0), '...  10.9 us
    unnamed x25, local copies, waits for them, and re-layouts  9.57 us
  transfers between devices with their start and end apart: 3, of which 3 were waited for; matrix products, arithmetic and copies ran while one was open for 0% of the time, Pallas kernels for 0%

profile of v1, /device:TPU:1, one launch (start us, length us, event | category | flops | bytes accessed | tf_op | source)
XLA Modules:
  0.0 351.8 jit_solution(1371453279640389816)
XLA Ops:
  6.5 0.0 copy-start
  6.5 0.0 all-gather.6.cloned.1.call-start
  6.5 0.8 convert_reduce_fusion
  7.4 1.2 convolution_convert_fusion
  8.6 0.5 copy.55
  9.2 48.1 %all_to_all.15 = bf16[32,2,4096]{2,1,0:T(2,128)(2,1)S(1)} all-to-all(bf16[32,2,4096]{2,1,0:T(2,128)(2,1)S(1)} %copy.55), channel_id=1, replica_groups=mesh['expert'=32,'fsdp'=16] {'expert'}, dimensions={0} | all-to-all | bytes 1048576 | tf_op jit(solution)/shard_map/all_to_all | solution.py:30
  57.3 1.1 copy.56
  58.4 0.0 all-gather.6.cloned.1.call-update
  58.4 0.0 all-gather.4.cloned.1.call-start
  58.5 82.3 %all-gather.6.cloned.1.call-done = bf16[512,2,4096]{2,0,1:T(8,128)(2,1)} async-done(((bf16[32,2,4096]{2,0,1:T(8,128)(2,1)}), bf16[512,2,4096]{2,0,1:T(8,128)(2,1)}) %all-gather.6.cloned.1.call-update) | async-done | bytes 8388624 | tf_op jit(solution)/shard_map/all_gather | solution.py:31
  140.8 0.0 copy-start.3
  140.8 0.0 copy-start.4
  140.8 6.0 %fusion.10 = f32[16,32,1,2,96]{4,1,3,0,2:T(8,128)S(1)} fusion(bf16[16,32,2,4096]{3,1,0,2:T(8,128)(2,1)} %bitcast.157, bf16[1,96,4096]{2,1,0:T(8,128)(2,1)} %param.9), kind=kOutput, calls=%fused_computation.10 | convolution fusion | flops 805306368 | bytes 9568256 | tf_op jit(solution)/shard_map/knjcd,jhd->knjch/dot_general | solution.py:33
  146.8 0.0 copy-done.3
  146.8 0.1 copy-done.4
  146.9 2.3 fusion.19
  149.3 2.1 copy.59
  151.3 0.0 all-gather.4.cloned.1.call-update
  151.4 103.8 %all-gather.4.cloned.1.call-done = bf16[16,32,1,2,1536]{1,0,3,2,4:T(8,128)(2,1)} async-done(((bf16[16,32,1,2,96]{1,0,3,2,4:T(8,128)(2,1)}), bf16[16,32,1,2,1536]{1,0,3,2,4:T(8,128)(2,1)}) %all-gather.4.cloned.1.call-update) | async-done | bytes 3145744 | tf_op jit(solution)/shard_map/all_gather | solution.py:38
  255.2 13.4 %copy.60 = bf16[16,32,1,2,1536]{4,1,3,0,2:T(8,128)(2,1)} copy(bf16[16,32,1,2,1536]{1,0,3,2,4:T(8,128)(2,1)} %all-gather.4.cloned.1.call-done) | data formatting | bytes 6291456 | tf_op jit(solution)/shard_map/all_gather | solution.py:38
  268.6 0.0 copy-done
  268.6 0.0 copy-start.2
  268.6 0.0 copy-start.1
  268.6 2.9 fusion.7
  271.5 0.5 copy.61
  272.0 44.3 %all_to_all.16 = bf16[16,32,2,256]{3,2,0,1:T(2,128)(2,1)S(1)} all-to-all(bf16[16,32,2,256]{3,2,0,1:T(2,128)(2,1)S(1)} %copy.61), channel_id=1, replica_groups=mesh['expert'=32,'fsdp'=16] {'expert'}, dimensions={1} | all-to-all | bytes 1048576 | tf_op jit(solution)/shard_map/all_to_all | solution.py:45
  316.4 0.6 constant_dynamic-update-slice_fusion.15
  317.0 0.6 constant_dynamic-update-slice_fusion.14
  317.6 0.6 constant_dynamic-update-slice_fusion.13
  318.3 0.6 constant_dynamic-update-slice_fusion.12
  318.9 0.6 constant_dynamic-update-slice_fusion.11
  319.5 0.6 constant_dynamic-update-slice_fusion.10
  320.2 0.6 constant_dynamic-update-slice_fusion.9
  320.8 0.6 constant_dynamic-update-slice_fusion.8
  321.4 0.6 constant_dynamic-update-slice_fusion.7
  322.1 0.6 constant_dynamic-update-slice_fusion.6
  322.7 0.6 constant_dynamic-update-slice_fusion.5
  323.3 0.6 constant_dynamic-update-slice_fusion.4
  324.0 0.6 constant_dynamic-update-slice_fusion.3
  324.6 0.6 constant_dynamic-update-slice_fusion.2
  325.2 0.6 constant_dynamic-update-slice_fusion.1
  325.8 0.6 constant_dynamic-update-slice_fusion
  326.5 5.8 %all-to-all-start.2 = ((bf16[16,1,32,2,256]{4,3,2,1,0:T(2,128)(2,1)}), bf16[16,1,32,2,256]{4,3,2,1,0:T(2,128)(2,1)S(1)}, u32[]{:S(2)}, u32[]{:S(2)}) async-start(bf16[16,1,32,2,256]{4,3,2,1,0:T(2,128)(2,1)} %constant_dynamic-update-slice_fusion), calls=%async_computation.2 | async-start | bytes 1048576 | tf_op jit(solution)/shard_map/all_to_all | solution.py:47
  332.2 0.0 copy-done.2
  332.2 0.1 reduce_sum.28
  332.4 0.1 broadcast_divide_fusion
  332.4 0.0 copy-done.1
  332.4 0.1 fusion.27
  332.5 10.9 %all-to-all-done.2 = bf16[16,1,32,2,256]{4,3,2,1,0:T(2,128)(2,1)S(1)} async-done(((bf16[16,1,32,2,256]{4,3,2,1,0:T(2,128)(2,1)}), bf16[16,1,32,2,256]{4,3,2,1,0:T(2,128)(2,1)S(1)}, u32[]{:S(2)}, u32[]{:S(2)}) %all-to-all-start.2) | async-done | bytes 524320 | tf_op jit(solution)/shard_map/all_to_all | solution.py:47
  343.4 0.3 copy.77
  343.7 0.2 reshape_reshape.3
  343.9 1.0 fusion.4
  (3 shorter events, 0.0 us)
Async XLA Ops:
  6.5 262.1 %copy-start = (bf16[1,1536,256]{2,1,0:T(8,128)(2,1)S(1)}, bf16[1,1536,256]{2,1,0:T(8,128)(2,1)}, u32[]{:S(2)}) copy-start(bf16[1,1536,256]{2,1,0:T(8,128)(2,1)} %param.11) | copy-start | bytes 2359300
  6.5 134.3 %all-gather.6.cloned.1.call-start = ((), (), s32[]{:S(2)}) async-start(), calls=%async_computation.4 | async-start | bytes 8912896 | tf_op jit(solution)/shard_map/all_gather | solution.py:31
  58.4 196.7 %all-gather.4.cloned.1.call-start = ((), (), s32[]{:S(2)}) async-start(), calls=%async_computation.3 | async-start | bytes 13369344 | tf_op jit(solution)/shard_map/all_gather | solution.py:38
  140.8 6.0 %copy-start.3 = (bf16[512,2,4096]{2,0,1:T(8,128)(2,1)S(1)}, bf16[512,2,4096]{2,0,1:T(8,128)(2,1)}, u32[]{:S(2)}) copy-start(bf16[512,2,4096]{2,0,1:T(8,128)(2,1)} %all-gather.6.cloned.1.call-done) | copy-start | bytes 25165828
  140.8 6.1 %copy-start.4 = (bf16[1,96,4096]{2,1,0:T(8,128)(2,1)S(1)}, bf16[1,96,4096]{2,1,0:T(8,128)(2,1)}, u32[]{:S(2)}) copy-start(bf16[1,96,4096]{2,1,0:T(8,128)(2,1)} %param.10) | copy-start | bytes 2359300
  268.6 63.7 %copy-start.2 = (f32[7,8]{1,0:T(8,128)S(1)}, f32[7,8]{1,0:T(8,128)}, u32[]{:S(2)}) copy-start(f32[7,8]{1,0:T(8,128)} %param.8) | copy-start | bytes 676
  268.6 63.9 %copy-start.1 = (s32[7,8]{1,0:T(8,128)S(1)}, s32[7,8]{1,0:T(8,128)}, u32[]{:S(2)}) copy-start(s32[7,8]{1,0:T(8,128)} %param.7) | copy-start | bytes 676
  326.5 16.9 %all-to-all-start.2 = ((bf16[16,1,32,2,256]{4,3,2,1,0:T(2,128)(2,1)}), bf16[16,1,32,2,256]{4,3,2,1,0:T(2,128)(2,1)S(1)}, u32[]{:S(2)}, u32[]{:S(2)}) async-start(bf16[16,1,32,2,256]{4,3,2,1,0:T(2,128)(2,1)} %constant_dynamic-update-slice_fusion), calls=%async_computation.2 | async-start | bytes 1048576 | tf_op jit(solution)/shard_map/all_to_all | solution.py:47
Sparse Core Ops, SparseCore 0:
  58.6 82.1 all-gather.5
  151.5 103.6 all-gather.3
